TPU v7x, 32 devices: a whole 2x2x4 slice. The times are simulated.
32 devices in a mesh: groups: 2 (over y), ctx: 4 (over z), head: 2 (over x), sub: 2 (over core).
Axes of the slice: x: 2, y: 2, z: 4, core: 2. Of those that a mesh axis runs over, the one named last changes fastest.
Arguments:
- queries: bfloat16 [2048, 4096], P(('groups', 'ctx'), ('head', 'sub')), parts along dimension 0, may hold values from -24 to 24
- keys: bfloat16 [2048, 4096], P(('groups', 'ctx'), ('head', 'sub')), parts along dimension 0, may hold values from -24 to 24
- values: bfloat16 [2048, 4096], P(('groups', 'ctx'), ('head', 'sub')), parts along dimension 0, may hold values from -6 to 6
- mem_queries: bfloat16 [512, 4096], P('groups', ('head', 'sub')), parts along dimension 0, may hold values from -24 to 24
- mem_keys: bfloat16 [512, 4096], P('groups', ('head', 'sub')), parts along dimension 0, may hold values from -9 to 9
- mem_values: bfloat16 [512, 4096], P('groups', ('head', 'sub')), parts along dimension 0, may hold values from -6 to 6
- window_blocks: int32 [32, 5], P(('groups', 'ctx')), parts along dimension 0, may hold values from 0 to 15, as said below
- memory_blocks: int32 [32, 3], P(('groups', 'ctx')), parts along dimension 0, may hold values from 0 to 3, as said below
Outputs:
- attended: bfloat16 [2048, 4096], P(('groups', 'ctx'), ('head', 'sub')), parts along dimension 0
- memory_out: bfloat16 [512, 4096], P(('groups', 'ctx'), ('head', 'sub')), parts along dimension 0
There are 2 independent parts, one for each index of `groups`. A program takes and returns all parts, laid end to end along the dimension named above; each array names one. Nothing has to cross between parts.
Inputs may be any that keep to these rules, and one draw needn't show every extreme that they name: `window_blocks`: entry [b, 0] is b itself; the 5 entries of row b are distinct blocks within 4 blocks of b. `memory_blocks`: each row holds 3 distinct memory blocks in increasing order.
All inputs are finite; a program needn't handle non-finite values.
Results may differ from a plain program's by a relative error of at most 0.004.
Values may be sent and summed in bfloat16 or wider, within the bound.
A program may use at most 128 MiB of HBM per device.

v0:
```python
import math

import jax
import jax.numpy as jnp
from jax import lax
from jax.sharding import PartitionSpec as P

HD = 128
MEM = 256
BLK = 64
RADIUS = 4


def with_halo(block, sides, width):
    for axis, dim in sides:
        count = lax.axis_size(axis)
        forward = [(i, i + 1) for i in range(count - 1)]
        backward = [(target, source) for source, target in forward]
        low = lax.ppermute(
            lax.slice_in_dim(block, block.shape[dim] - width, None, axis=dim), axis, forward
        )
        high = lax.ppermute(lax.slice_in_dim(block, 0, width, axis=dim), axis, backward)
        block = jnp.concatenate([low, block, high], axis=dim)
    return block


def joined_2(value, axis, join):
    pieces = jax.tree.map(lambda part: lax.all_gather(part, axis), value)
    head = jax.tree.map(lambda part: part[0], pieces)
    tail = jax.tree.map(lambda part: part[1:], pieces)
    total, _ = lax.scan(lambda total, slab: (join(total, slab), None), head, tail)
    return total


def spread_factor_scale(partial_value, factors):
    return (partial_value.reshape(factors.shape + (-1,)) * factors[..., None]).reshape(
        partial_value.shape
    )


def combine_partials(first_part, second_part):
    first_peak, first_total, first_sum = first_part
    second_peak, second_total, second_sum = second_part
    joined = jnp.maximum(first_peak, second_peak)
    first_factor = jnp.exp(first_peak - joined)
    second_factor = jnp.exp(second_peak - joined)
    totals = first_total * first_factor + second_total * second_factor
    sums = spread_factor_scale(first_sum, first_factor) + spread_factor_scale(
        second_sum, second_factor
    )
    return (joined, totals, sums)


def on_device(
    queries, keys, values, mem_queries, mem_keys, mem_values, window_blocks, memory_blocks
):
    token_rows, columns = queries.shape
    head_count = columns // HD
    local_blocks = token_rows // BLK
    score_scale = 1.0 / math.sqrt(HD)
    halo_rows = RADIUS * BLK
    paired = jnp.stack([keys, values])
    extended = with_halo(paired, (("ctx", 1),), halo_rows)
    extended = extended.reshape(2, local_blocks + 2 * RADIUS, BLK, head_count, HD)
    first_block = lax.axis_index("ctx") * local_blocks
    local_index = window_blocks - first_block + RADIUS
    near_tiles = jnp.take(extended, local_index, axis=1)
    memory_pair = jnp.stack([mem_keys, mem_values]).reshape(2, MEM // BLK, BLK, head_count, HD)
    memory_tiles = jnp.take(memory_pair, memory_blocks, axis=1)
    slot_count = near_tiles.shape[2] + memory_tiles.shape[2]
    key_tiles = jnp.concatenate([near_tiles, memory_tiles], axis=2).reshape(
        2, local_blocks, slot_count * BLK, head_count, HD
    )
    query_rows = queries.reshape(local_blocks, BLK, head_count, HD)
    scores = (
        jnp.einsum("nqhd,nkhd->nhqk", query_rows, key_tiles[0], preferred_element_type=jnp.float32)
        * score_scale
    )
    highest = jnp.max(scores, axis=3, keepdims=True)
    exps = jnp.exp(scores - highest)
    totals = jnp.sum(exps, axis=3, keepdims=True)
    weights = exps.astype(jnp.bfloat16)
    summed = jnp.einsum(
        "nhqk,nkhd->nqhd", weights, key_tiles[1], preferred_element_type=jnp.float32
    )
    attended = (
        (summed / totals.transpose(0, 2, 1, 3)).reshape(token_rows, columns).astype(jnp.bfloat16)
    )
    memory_query_rows = mem_queries.reshape(MEM, head_count, HD)
    key_head_stack = keys.reshape(token_rows, head_count, HD)
    value_heads = values.reshape(token_rows, head_count, HD)
    memory_scores = (
        jnp.einsum(
            "rcp,xcp->rcx", memory_query_rows, key_head_stack, preferred_element_type=jnp.float32
        )
        * score_scale
    )
    memory_peak = jnp.max(memory_scores, axis=2)
    memory_exponents = jnp.exp(memory_scores - memory_peak[..., None])
    memory_total = jnp.sum(memory_exponents, axis=2)
    memory_sum = jnp.einsum(
        "vfi,ifr->vfr",
        memory_exponents.astype(jnp.bfloat16),
        value_heads,
        preferred_element_type=jnp.float32,
    ).reshape(MEM, columns)
    own_rows = MEM // lax.axis_size("ctx")
    row_start = lax.axis_index("ctx") * own_rows
    peak_all, total_all, sum_all = joined_2(
        (memory_peak, memory_total, memory_sum), "ctx", combine_partials
    )
    own_peak = lax.dynamic_slice_in_dim(peak_all, row_start, own_rows, 0)
    own_total = lax.dynamic_slice_in_dim(total_all, row_start, own_rows, 0)
    own_sum = lax.dynamic_slice_in_dim(sum_all, row_start, own_rows, 0)
    local_query_rows = lax.dynamic_slice_in_dim(memory_query_rows, row_start, own_rows, 0)
    memory_key_heads = mem_keys.reshape(MEM, head_count, HD)
    memvalue_heads = mem_values.reshape(MEM, head_count, HD)
    self_scores = (
        jnp.einsum(
            "bet,vet->bev", local_query_rows, memory_key_heads, preferred_element_type=jnp.float32
        )
        * score_scale
    )
    final_peak = jnp.maximum(own_peak, jnp.max(self_scores, axis=2))
    carried = jnp.exp(own_peak - final_peak)
    self_exps = jnp.exp(self_scores - final_peak[..., None])
    final_total = own_total * carried + jnp.sum(self_exps, axis=2)
    self_sum = jnp.einsum(
        "pte,ety->pty",
        self_exps.astype(jnp.bfloat16),
        memvalue_heads,
        preferred_element_type=jnp.float32,
    )
    merged = own_sum.reshape(own_rows, head_count, HD) * carried[..., None] + self_sum
    memory_out = (merged / final_total[..., None]).reshape(own_rows, columns).astype(jnp.bfloat16)
    return (attended, memory_out)


def solution(mesh):
    in_specs = (
        P(("groups", "ctx"), ("head", "sub")),
        P(("groups", "ctx"), ("head", "sub")),
        P(("groups", "ctx"), ("head", "sub")),
        P("groups", ("head", "sub")),
        P("groups", ("head", "sub")),
        P("groups", ("head", "sub")),
        P(("groups", "ctx"), None),
        P(("groups", "ctx"), None),
    )
    out_specs = (P(("groups", "ctx"), ("head", "sub")), P(("groups", "ctx"), ("head", "sub")))
    return jax.shard_map(
        on_device, mesh=mesh, in_specs=in_specs, out_specs=out_specs, check_vma=False
    )
```

profile of v0, /device:TPU:0, one launch (start us, length us, event | category | flops | bytes accessed | tf_op | source)
XLA Modules:
  0.0 172.0 jit_solution(52250200214364221)
XLA Ops:
  8.5 2.2 %copy.55 = bf16[256,1024]{0,1:T(8,128)(2,1)} copy(bf16[256,1024]{1,0:T(8,128)(2,1)} %param.12) | data formatting | bytes 1048576 | tf_op jit(solution)/shard_map/reshape | solution.py:91
  10.7 1.5 bitcast_reduce_fusion.1
  12.2 2.6 %fusion.22 = f32[8,256,128]{1,2,0:T(8,128)} fusion(bf16[256,8,128]{0,2,1:T(8,128)(2,1)} %bitcast.175, f32[8,256,256]{2,1,0:T(8,128)S(1)} %get-tuple-element.71, f32[256,8]{0,1:T(8,128)S(1)} %get-tuple-element.70), kind=kOutput, calls=%fused_computation.39 | convolution fusion | flops 135790592 | bytes 3678208 | tf_op jit(solution)/shard_map/vfi,ifr->vfr/dot_general | solution.py:101
  14.8 2.6 %copy.47 = f32[1,256,1024]{2,1,0:T(8,128)} copy(f32[1,256,1024]{1,2,0:T(8,128)} %bitcast.169) | data formatting | bytes 2097152 | tf_op jit(solution)/shard_map/all_gather;reshape | solution.py:28
  19.9 6.5 %collective-permute-start = (bf16[2,256,1024]{2,1,0:T(8,128)(2,1)}, bf16[2,256,1024]{2,1,0:T(8,128)(2,1)}, u32[]{:S(2)}, u32[]{:S(2)}) collective-permute-start(bf16[2,256,1024]{2,1,0:T(8,128)(2,1)} %pad_maximum_fusion.2), channel_id=1, source_target_pairs={{0,4},{4,8},{8,12},{1,5},{5,9},{9,13},{2,6},{6,10},{10,14},{3,7},{... | collective-permute-start | bytes 3145736 | tf_op jit(solution)/shard_map/ppermute | solution.py:19
  26.4 74.3 %all-gather = f32[1024,8]{0,1:T(8,128)S(1)} all-gather(f32[256,8]{0,1:T(8,128)S(1)} %get-tuple-element.70), channel_id=2, replica_groups=mesh['groups'=2,'ctx'=4,'head'=2,'sub'=2] {'ctx'}, dimensions={0}, use_global_device_ids=true | all-gather | bytes 40960 | tf_op jit(solution)/shard_map/all_gather | solution.py:28
  101.1 13.6 %all-gather.1 = f32[1024,8]{0,1:T(8,128)S(1)} all-gather(f32[256,8]{0,1:T(8,128)S(1)} %fusion.13), channel_id=3, replica_groups=mesh['groups'=2,'ctx'=4,'head'=2,'sub'=2] {'ctx'}, dimensions={0}, use_global_device_ids=true | all-gather | bytes 40960 | tf_op jit(solution)/shard_map/all_gather | solution.py:28
  114.7 1.9 %copy.66 = bf16[32,8,8,128]{3,2,1,0:T(8,128)(2,1)} copy(bf16[32,8,8,128]{3,1,2,0:T(8,128)(2,1)} %bitcast.180) | data formatting | bytes 1048576
  116.7 1.9 %copy.65 = bf16[32,8,8,128]{3,2,1,0:T(8,128)(2,1)} copy(bf16[32,8,8,128]{3,1,2,0:T(8,128)(2,1)} %bitcast.173) | data formatting | bytes 1048576
  118.7 2.0 %copy.67 = bf16[32,8,8,128]{3,2,1,0:T(8,128)(2,1)} copy(bf16[32,8,8,128]{3,1,2,0:T(8,128)(2,1)} %bitcast.179) | data formatting | bytes 1048576
  120.7 1.4 pad_maximum_fusion.3
  122.1 2.7 %gather_fusion.1 = bf16[12,2,64,8,128]{4,3,2,1,0:T(8,128)(2,1)} fusion(bf16[2,4,64,8,128]{4,3,2,1,0:T(8,128)(2,1)S(1)} %pad_maximum_fusion.3, s32[1024]{0:T(1024)S(1)} %pad_clamp_fusion), kind=kCustom, calls=%fused_computation.1 | custom fusion | bytes 6291504 | tf_op jit(solution)/shard_map/jit(_take)/gather | solution.py:69
  126.1 3.9 %select_bitcast_fusion.1 = bf16[2,4,3,64,8,128]{5,4,3,0,2,1:T(8,128)(2,1)} fusion(bf16[4,3,2,64,8,128]{5,4,3,2,1,0:T(8,128)(2,1)} %bitcast.163, pred[4,3]{1,0:T(4,128)(4,1)S(1)} %compare_and_fusion), kind=kLoop, calls=%fused_computation.22 | loop fusion | flops 1572864 | bytes 6291468 | tf_op jit(solution)/shard_map/jit(_take)/select_n | solution.py:69
  130.0 1.8 %pad_maximum_fusion.1 = bf16[2,768,1024]{2,1,0:T(8,128)(2,1)S(1)} fusion(bf16[2,256,1024]{2,1,0:T(8,128)(2,1)} %collective-permute-done.1, bf16[1,256,1024]{2,1,0:T(8,128)(2,1)S(1)} %bitcast.166, bf16[1,256,1024]{2,1,0:T(8,128)(2,1)S(1)} %bitcast.168, bf16[2,256,1024]{2,1,0:T(8,128)(2,1)} %collective-permute-done), kind=kLoop, calls=%fused_computation.21 | loop fusion | flops 12582912 | bytes 6291456 | tf_op jit(solution)/shard_map/concatenate | solution.py:23
  132.6 4.1 %gather_fusion = bf16[20,2,64,8,128]{4,3,2,1,0:T(8,128)(2,1)} fusion(bf16[2,12,64,8,128]{4,3,2,1,0:T(8,128)(2,1)S(1)} %bitcast.160, s32[1024]{0:T(1024)S(1)} %pad_clamp_fusion.1), kind=kCustom, calls=%fused_computation | custom fusion | bytes 10485840 | tf_op jit(solution)/shard_map/jit(_take)/gather | solution.py:67
  136.7 3.2 %select_bitcast_fusion = bf16[2,4,5,64,8,128]{5,4,3,0,2,1:T(8,128)(2,1)S(1)} fusion(bf16[4,5,2,64,8,128]{5,4,3,2,1,0:T(8,128)(2,1)} %bitcast.161, pred[4,5]{1,0:T(4,128)(4,1)S(1)} %get-tuple-element.64), kind=kLoop, calls=%fused_computation.13 | loop fusion | flops 2621440 | bytes 10485780 | tf_op jit(solution)/shard_map/jit(_take)/select_n | solution.py:67
  143.2 1.6 bitcast_reduce_fusion
  146.1 1.6 divide_convert_fusion
  149.0 1.3 slice_bitcast_fusion
  150.4 3.9 %slice.49 = f32[3,256,1024]{2,1,0:T(8,128)} slice(f32[4,256,1024]{2,1,0:T(8,128)} %all-gather.4.cloned.1.call-done), slice={[1:4], [0:256], [0:1024]} | slice | bytes 6291456 | tf_op jit(solution)/shard_map/slice | solution.py:30
  154.3 9.4 %while.14 = (s32[]{:T(128)}, f32[256,8]{0,1:T(8,128)S(1)}, f32[256,8]{0,1:T(8,128)S(1)}, f32[256,1024]{1,0:T(8,128)S(1)}, f32[3,256,8]{1,2,0:T(8,128)S(1)}, /*in...) while((s32[]{:T(128)}, f32[256,8]{0,1:T(8,128)S(1)}, f32[256,8]{0,1:T(8,128)S(1)}, ...), condition=%wide.region_5.6_spmd, body=%wide.region_4.5_spmd.sunk | while | flops 798722 | bytes 7454821 | solution.py:31
  155.3 2.2 %fusion.57 = f32[256,1024]{1,0:T(8,128)S(1)} fusion(f32[32,8,8,128]{3,2,1,0:T(8,128)S(1)} %bitcast.158, f32[256,1024]{1,0:T(8,128)S(1)} %get-tuple-element.136, f32[32,8,8,128]{3,2,1,0:T(8,128)S(1)} %bitcast.159, f32[3,256,1024]{2,1,0:T(8,128)} %get-tuple-element.147, s32[]{:T(128)S(6)} %copy.108), kind=kLoop, calls=%fused_computation.3.clone.1 | loop fusion | flops 786432 | bytes 5242884 | tf_op jit(solution)/shard_map/while/body/eval_jaxpr/add | solution.py:48
  158.4 2.2 %fusion.57 = f32[256,1024]{1,0:T(8,128)S(1)} fusion(f32[32,8,8,128]{3,2,1,0:T(8,128)S(1)} %bitcast.158, f32[256,1024]{1,0:T(8,128)S(1)} %get-tuple-element.136, f32[32,8,8,128]{3,2,1,0:T(8,128)S(1)} %bitcast.159, f32[3,256,1024]{2,1,0:T(8,128)} %get-tuple-element.147, s32[]{:T(128)S(6)} %copy.108), kind=kLoop, calls=%fused_computation.3.clone.1 | loop fusion | flops 786432 | bytes 5242884 | tf_op jit(solution)/shard_map/while/body/eval_jaxpr/add | solution.py:48
  161.5 2.2 %fusion.57 = f32[256,1024]{1,0:T(8,128)S(1)} fusion(f32[32,8,8,128]{3,2,1,0:T(8,128)S(1)} %bitcast.158, f32[256,1024]{1,0:T(8,128)S(1)} %get-tuple-element.136, f32[32,8,8,128]{3,2,1,0:T(8,128)S(1)} %bitcast.159, f32[3,256,1024]{2,1,0:T(8,128)} %get-tuple-element.147, s32[]{:T(128)S(6)} %copy.108), kind=kLoop, calls=%fused_computation.3.clone.1 | loop fusion | flops 786432 | bytes 5242884 | tf_op jit(solution)/shard_map/while/body/eval_jaxpr/add | solution.py:48
  (76 shorter events, 16.4 us)
Async XLA Ops:
  7.2 141.9 %all-gather.4.cloned.1.call-start = ((), (), s32[]{:S(2)}) async-start(), calls=%async_computation | async-start | bytes 5242880 | tf_op jit(solution)/shard_map/all_gather | solution.py:28
  8.5 2.2 %copy-start.3 = (bf16[256,1024]{0,1:T(8,128)(2,1)}, bf16[256,1024]{0,1:T(8,128)(2,1)S(1)}, u32[]{:S(2)}) copy-start(bf16[256,1024]{0,1:T(8,128)(2,1)S(1)} %copy.42) | copy-start | bytes 1572868
  12.2 5.3 %copy-start.1 = (bf16[256,1024]{1,0:T(8,128)(2,1)S(1)}, bf16[256,1024]{1,0:T(8,128)(2,1)}, u32[]{:S(2)}) copy-start(bf16[256,1024]{1,0:T(8,128)(2,1)} %param.12) | copy-start | bytes 1572868
  12.2 5.3 %copy-start.2 = (bf16[256,1024]{1,0:T(8,128)(2,1)S(1)}, bf16[256,1024]{1,0:T(8,128)(2,1)}, u32[]{:S(2)}) copy-start(bf16[256,1024]{1,0:T(8,128)(2,1)} %param.11) | copy-start | bytes 1572868
  14.8 99.8 %copy-start.12 = (s32[4,5]{1,0:T(4,128)S(1)}, s32[4,5]{1,0:T(4,128)}, u32[]{:S(2)}) copy-start(s32[4,5]{1,0:T(4,128)} %param.16) | copy-start | bytes 244
  17.5 101.2 %copy-start.11 = (s32[4,3]{1,0:T(4,128)S(1)}, s32[4,3]{1,0:T(4,128)}, u32[]{:S(2)}) copy-start(s32[4,3]{1,0:T(4,128)} %param.17) | copy-start | bytes 148
  18.6 111.4 %collective-permute-start.1 = (bf16[2,256,1024]{2,1,0:T(8,128)(2,1)}, bf16[2,256,1024]{2,1,0:T(8,128)(2,1)}, u32[]{:S(2)}, u32[]{:S(2)}) collective-permute-start(bf16[2,256,1024]{2,1,0:T(8,128)(2,1)} %pad_maximum_fusion.2), channel_id=1, source_target_pairs={{4,0},{8,4},{12,8},{5,1},{9,5},{13,9},{6,2},{10,6},{14,10},{7,3},{... | collective-permute-start | bytes 3145736 | tf_op jit(solution)/shard_map/ppermute | solution.py:22
  19.9 110.1 %collective-permute-start = (bf16[2,256,1024]{2,1,0:T(8,128)(2,1)}, bf16[2,256,1024]{2,1,0:T(8,128)(2,1)}, u32[]{:S(2)}, u32[]{:S(2)}) collective-permute-start(bf16[2,256,1024]{2,1,0:T(8,128)(2,1)} %pad_maximum_fusion.2), channel_id=1, source_target_pairs={{0,4},{4,8},{8,12},{1,5},{5,9},{9,13},{2,6},{6,10},{10,14},{3,7},{... | collective-permute-start | bytes 3145736 | tf_op jit(solution)/shard_map/ppermute | solution.py:19
  100.7 24.1 %copy-start.9 = (f32[1024,8]{0,1:T(8,128)}, f32[1024,8]{0,1:T(8,128)S(1)}, u32[]{:S(2)}) copy-start(f32[1024,8]{0,1:T(8,128)S(1)} %all-gather) | copy-start | bytes 98308
  114.6 10.1 %copy-start.10 = (f32[1024,8]{0,1:T(8,128)}, f32[1024,8]{0,1:T(8,128)S(1)}, u32[]{:S(2)}) copy-start(f32[1024,8]{0,1:T(8,128)S(1)} %all-gather.1) | copy-start | bytes 98308
  120.7 4.1 %copy-start.4 = (bf16[256,1024]{0,1:T(8,128)(2,1)S(1)}, bf16[256,1024]{0,1:T(8,128)(2,1)}, u32[]{:S(2)}) copy-start(bf16[256,1024]{0,1:T(8,128)(2,1)} %copy-done.3) | copy-start | bytes 1572868
  120.7 4.1 %copy-start.5 = (bf16[256,1024]{1,0:T(8,128)(2,1)S(1)}, bf16[256,1024]{1,0:T(8,128)(2,1)}, u32[]{:S(2)}) copy-start(bf16[256,1024]{1,0:T(8,128)(2,1)} %param.14) | copy-start | bytes 1572868
  136.7 3.4 %copy-start = (bf16[2,4,3,64,8,128]{5,4,3,0,2,1:T(8,128)(2,1)S(1)}, bf16[2,4,3,64,8,128]{5,4,3,0,2,1:T(8,128)(2,1)}, u32[]{:S(2)}) copy-start(bf16[2,4,3,64,8,128]{5,4,3,0,2,1:T(8,128)(2,1)} %select_bitcast_fusion.1) | copy-start | bytes 9437188
  142.0 1.1 copy-start.7
  149.0 5.3 %slice-start = ((f32[1024,8]{0,1:T(8,128)}), f32[768,8]{0,1:T(8,128)S(1)}, s32[]{:S(2)}) async-start(f32[1024,8]{0,1:T(8,128)} %copy-done.9), calls=%async_computation.1 | async-start | bytes 49152 | tf_op jit(solution)/shard_map/slice | solution.py:30
  149.0 5.3 %slice-start.1 = ((f32[1024,8]{0,1:T(8,128)}), f32[768,8]{0,1:T(8,128)S(1)}, s32[]{:S(2)}) async-start(f32[1024,8]{0,1:T(8,128)} %copy-done.10), calls=%async_computation.2 | async-start | bytes 49152 | tf_op jit(solution)/shard_map/slice | solution.py:30
  154.3 9.5 %copy-start.6 = (f32[64,8,256]{2,0,1:T(8,128)S(1)}, f32[64,8,256]{2,0,1:T(8,128)}, u32[]{:S(2)}) copy-start(f32[64,8,256]{2,0,1:T(8,128)} %get-tuple-element.73) | copy-start | bytes 1572868
  154.3 9.9 %copy-start.8 = (bf16[256,1024]{1,0:T(8,128)(2,1)S(1)}, bf16[256,1024]{1,0:T(8,128)(2,1)}, u32[]{:S(2)}) copy-start(bf16[256,1024]{1,0:T(8,128)(2,1)} %param.15) | copy-start | bytes 1572868
Sparse Core Ops, SparseCore 0:
  17.6 99.3 all-gather.3
where the time goes:
time: 173 us; the launch traced here: 172 us
  blocking collectives  87.8 us (51%)
  local copies, waits for them, and re-layouts  32.2 us (19%)
  other arithmetic  20.8 us (12%)
  between operations  14.3 us (8%)
  matrix products  8.99 us (5%)
  starting transfers between devices  7.85 us (5%)
    all_gather x2, blocking collectives, joined_2(): pieces = jax.tree.map(lambda part: lax.all_gather(part, axis), value)  87.8 us
    unnamed x32, local copies, waits for them, and re-layouts  9.08 us
    ppermute x1, starting transfers between devices, with_halo(): lax.ppermute(lax.slice_in_dim(block, block.shape[dim] - width, None, axis...  6.53 us
    add x3, other arithmetic, combine_partials(): spread_factor_scale(first_sum, first_factor)  6.47 us
    gather x1, local copies, waits for them, and re-layouts, on_device(): near_tiles = jnp.take(extended, local_index, axis=1)  4.08 us
    slice x5, local copies, waits for them, and re-layouts, joined_2(): tail = jax.tree.map(lambda part: part[1:], pieces)  3.94 us
    select_n x2, other arithmetic, on_device(): memory_tiles = jnp.take(memory_pair, memory_blocks, axis=1)  3.9 us
  transfers between devices with their start and end apart: 3, of which 0 were waited for; matrix products, arithmetic and copies ran while one was open for 21% of the time, Pallas kernels for 0%

commit v1 on v0

v1 whole, which is shorter than its diff:
```python
import functools
import math

import jax
import jax.numpy as jnp
from jax import lax
from jax.experimental import pallas as pl
from jax.experimental.pallas import tpu as pltpu
from jax.sharding import PartitionSpec as P

HD = 128
BLK = 64
RADIUS = 4
CHUNK_HEADS = 2
MESH = pl.DeviceIdType.MESH
EXPONENT_SCALE = math.log2(math.e) / math.sqrt(HD)
LOWEST = -1e30


def dot_nt(a, b):
    return lax.dot_general(a, b, (((1,), (1,)), ((), ())), preferred_element_type=jnp.float32)


def dot_nn(a, b):
    return lax.dot_general(a, b, (((1,), (0,)), ((), ())), preferred_element_type=jnp.float32)


def softmax_parts(scores):
    peak = jnp.max(scores, axis=1, keepdims=True)
    exps = jnp.exp2((scores - peak) * EXPONENT_SCALE)
    total = jnp.sum(exps, axis=1, keepdims=True)
    return peak, total, exps.astype(jnp.bfloat16)


def kernel(n, heads, rows, mem, chunks, *refs):
    (wb, mb, q_h, k_h, v_h, mq_h, mk_h, mv_h, out_h, mout_h) = refs[:10]
    refs = refs[10:]
    ext_k, ext_v, refs = refs[:chunks], refs[chunks : 2 * chunks], refs[2 * chunks :]
    (q_s, mq_s, mqo_s, mk_s, mv_s, out_s, mout_s, own_sum, own_stat, msg, msg_stat, got, got_stat) = refs[:13]
    (local_sem, kv_local, kv_send, kv_recv, p_send, p_recv, ps_send, ps_recv, out_sem) = refs[13:]

    per = heads // chunks
    width = per * HD
    own = mem // n
    blocks = rows // BLK
    halo = RADIUS * BLK
    me = lax.axis_index("ctx")
    has_low, has_high = me > 0, me < n - 1

    locals_ = [
        pltpu.make_async_copy(mq_h, mq_s, local_sem.at[0]),
        pltpu.make_async_copy(q_h, q_s, local_sem.at[1]),
        pltpu.make_async_copy(mk_h, mk_s, local_sem.at[2]),
        pltpu.make_async_copy(mv_h, mv_s, local_sem.at[3]),
        pltpu.make_async_copy(mq_h.at[pl.ds(pl.multiple_of(me * own, own), own)], mqo_s, local_sem.at[4]),
    ]
    kv_locals = []
    for c in range(chunks):
        cols = pl.ds(c * width, width)
        for t, (src, ext) in enumerate(((k_h, ext_k), (v_h, ext_v))):
            kv_locals.append(
                pltpu.make_async_copy(
                    src.at[:, :, cols], ext[c].at[pl.ds(RADIUS, blocks)], kv_local.at[c, t]
                )
            )
    locals_[0].start()
    for copy in kv_locals:
        copy.start()
    for copy in locals_[1:]:
        copy.start()

    barrier = pltpu.get_barrier_semaphore()
    for j in range(n):

        @pl.when(j != me)
        def _(j=j):
            pl.semaphore_signal(barrier, inc=1, device_id={"ctx": j}, device_id_type=MESH)

    pl.semaphore_wait(barrier, n - 1)

    high, low = jnp.minimum(me + 1, n - 1), jnp.maximum(me - 1, 0)

    def halo_copy(c, t, upward):
        src, ext = ((k_h, ext_k), (v_h, ext_v))[t]
        cols = pl.ds(c * width, width)
        d = 0 if upward else 1
        if upward:
            part, start, target = pl.ds(blocks - RADIUS, RADIUS), 0, high
        else:
            part, start, target = pl.ds(0, RADIUS), RADIUS + blocks, low
        return pltpu.make_async_remote_copy(
            src_ref=src.at[part, :, cols],
            dst_ref=ext[c].at[pl.ds(start, RADIUS)],
            send_sem=kv_send.at[c, t, d],
            recv_sem=kv_recv.at[c, t, d],
            device_id={"ctx": target},
            device_id_type=MESH,
        )

    def send_halo(c):
        @pl.when(has_high)
        def _():
            for t in range(2):
                halo_copy(c, t, True).start()

        @pl.when(has_low)
        def _():
            for t in range(2):
                halo_copy(c, t, False).start()

    early = (chunks + 1) // 2
    for c in range(early):
        send_halo(c)

    @pl.when(jnp.logical_not(has_low))
    def _():
        for c in range(chunks):
            ext_k[c][0:RADIUS] = jnp.zeros((RADIUS, BLK, width), jnp.bfloat16)
            ext_v[c][0:RADIUS] = jnp.zeros((RADIUS, BLK, width), jnp.bfloat16)

    @pl.when(jnp.logical_not(has_high))
    def _():
        for c in range(chunks):
            ext_k[c][RADIUS + blocks :] = jnp.zeros((RADIUS, BLK, width), jnp.bfloat16)
            ext_v[c][RADIUS + blocks :] = jnp.zeros((RADIUS, BLK, width), jnp.bfloat16)

    locals_[0].wait()
    lane = lax.broadcasted_iota(jnp.int32, (mem, HD), 1)
    stats = jnp.zeros((mem, HD), jnp.float32)
    for h in range(heads):
        c, o = h // per, (h % per) * HD
        if o == 0:
            kv_locals[2 * c].wait()
            kv_locals[2 * c + 1].wait()
        key = ext_k[c][RADIUS : RADIUS + blocks, :, o : o + HD].reshape(rows, HD)
        value = ext_v[c][RADIUS : RADIUS + blocks, :, o : o + HD].reshape(rows, HD)
        peak, total, weights = softmax_parts(dot_nt(mq_s[:, h * HD : (h + 1) * HD], key))
        part = dot_nn(weights, value) / total
        stats = jnp.where(lane == h, peak, stats)
        stats = jnp.where(lane == heads + h, total, stats)
        msg[:, :, h * HD : (h + 1) * HD] = part.reshape(n, own, HD).astype(jnp.bfloat16)
    stats = stats.reshape(n, own, HD)
    for j in range(n):
        msg_stat[j] = stats[j].T[: 2 * heads]

    def far(j):
        return jnp.logical_or(j - me >= 2, me - j >= 2)

    def partial_copies(slot, source, target):
        return (
            pltpu.make_async_remote_copy(
                src_ref=msg.at[slot],
                dst_ref=got.at[source],
                send_sem=p_send.at[slot],
                recv_sem=p_recv.at[source],
                device_id={"ctx": target},
                device_id_type=MESH,
            ),
            pltpu.make_async_remote_copy(
                src_ref=msg_stat.at[slot],
                dst_ref=got_stat.at[source],
                send_sem=ps_send.at[slot],
                recv_sem=ps_recv.at[source],
                device_id={"ctx": target},
                device_id_type=MESH,
            ),
        )

    for j in range(n):

        @pl.when(far(j))
        def _(j=j):
            for copy in partial_copies(j, me, j):
                copy.start()

    for c in range(early, chunks):
        send_halo(c)

    for copy in locals_[1:]:
        copy.wait()

    column = lax.broadcasted_iota(jnp.int32, (1, 2 * halo + rows + mem), 1)
    first = jnp.where(has_low, 0, halo)
    last = jnp.where(has_high, 2 * halo + rows, halo + rows)
    present = jnp.logical_or(
        jnp.logical_and(column >= first, column < last), column >= 2 * halo + rows
    )
    base = me * blocks - RADIUS

    def finish_memory(h):
        cols = slice(h * HD, (h + 1) * HD)
        mout_s[:, cols] = (own_sum[:, cols] / own_stat[:, heads + h : heads + h + 1]).astype(jnp.bfloat16)

    def fold(i, h):
        cols = slice(h * HD, (h + 1) * HD)
        columns = got_stat[i].T
        peak, total = own_stat[:, h : h + 1], own_stat[:, heads + h : heads + h + 1]
        other_peak, other_total = columns[:, h : h + 1], columns[:, heads + h : heads + h + 1]
        joined = jnp.maximum(peak, other_peak)
        factor = jnp.exp2((peak - joined) * EXPONENT_SCALE)
        other = other_total * jnp.exp2((other_peak - joined) * EXPONENT_SCALE)
        own_sum[:, cols] = own_sum[:, cols] * factor + got[i, :, cols].astype(jnp.float32) * other
        own_stat[:, h : h + 1] = joined
        own_stat[:, heads + h : heads + h + 1] = total * factor + other

    def fold_heads(some):
        for i in range(n):

            @pl.when(far(i))
            def _(i=i):
                for h in some:
                    fold(i, h)

        for h in some:
            finish_memory(h)

    for c in range(chunks):
        if c == chunks - 1:
            for i in range(n):

                @pl.when(far(i))
                def _(i=i):
                    for copy in partial_copies(i, i, i):
                        copy.wait_recv()

            fold_heads(range((chunks - 1) * per))

        @pl.when(has_low)
        def _(c=c):
            for t in range(2):
                halo_copy(c, t, True).wait_recv()

        @pl.when(has_high)
        def _(c=c):
            for t in range(2):
                halo_copy(c, t, False).wait_recv()

        for p in range(per):
            h, o = c * per + p, p * HD
            cols = slice(h * HD, (h + 1) * HD)
            for b in range(blocks):
                near = [
                    jnp.clip(wb[b, s] - base, 0, blocks + 2 * RADIUS - 1) for s in range(wb.shape[1])
                ]
                distant = [jnp.clip(mb[b, s], 0, mem // BLK - 1) for s in range(mb.shape[1])]
                key = jnp.concatenate(
                    [ext_k[c][s, :, o : o + HD] for s in near]
                    + [mk_s[s, :, cols] for s in distant],
                    axis=0,
                )
                value = jnp.concatenate(
                    [ext_v[c][s, :, o : o + HD] for s in near]
                    + [mv_s[s, :, cols] for s in distant],
                    axis=0,
                )
                part = slice(b * BLK, (b + 1) * BLK)
                peak, total, weights = softmax_parts(dot_nt(q_s[part, cols], key))
                out_s[part, cols] = (dot_nn(weights, value) / total).astype(jnp.bfloat16)
            query = mqo_s[:, cols]
            key = jnp.concatenate(
                [
                    ext_k[c][:, :, o : o + HD].reshape(rows + 2 * halo, HD),
                    mk_s[:, :, cols].reshape(mem, HD),
                ],
                axis=0,
            )
            value = jnp.concatenate(
                [
                    ext_v[c][:, :, o : o + HD].reshape(rows + 2 * halo, HD),
                    mv_s[:, :, cols].reshape(mem, HD),
                ],
                axis=0,
            )
            scores = jnp.where(present, dot_nt(query, key), LOWEST)
            peak, total, weights = softmax_parts(scores)
            own_sum[:, cols] = dot_nn(weights, value)
            own_stat[:, h : h + 1] = peak
            own_stat[:, heads + h : heads + h + 1] = total
        chunk_cols = pl.ds(c * width, width)
        pltpu.make_async_copy(out_s.at[:, chunk_cols], out_h.at[:, chunk_cols], out_sem.at[c]).start()

    fold_heads(range((chunks - 1) * per, heads))
    mem_out = pltpu.make_async_copy(mout_s, mout_h, out_sem.at[chunks])
    mem_out.start()

    for c in range(chunks):

        @pl.when(has_high)
        def _(c=c):
            for t in range(2):
                halo_copy(c, t, True).wait_send()

        @pl.when(has_low)
        def _(c=c):
            for t in range(2):
                halo_copy(c, t, False).wait_send()

    for j in range(n):

        @pl.when(far(j))
        def _(j=j):
            for copy in partial_copies(j, me, j):
                copy.wait_send()

    for c in range(chunks):
        chunk_cols = pl.ds(c * width, width)
        pltpu.make_async_copy(out_s.at[:, chunk_cols], out_h.at[:, chunk_cols], out_sem.at[c]).wait()
    mem_out.wait()


def on_device(
    n, queries, keys, values, mem_queries, mem_keys, mem_values, window_blocks, memory_blocks
):
    rows, columns = queries.shape
    mem = mem_queries.shape[0]
    heads = columns // HD
    chunks = heads // CHUNK_HEADS
    width = CHUNK_HEADS * HD
    own = mem // n
    ext_blocks = rows // BLK + 2 * RADIUS
    bf16, f32 = jnp.bfloat16, jnp.float32
    any_spec = pl.BlockSpec(memory_space=pl.ANY)
    smem_spec = pl.BlockSpec(memory_space=pltpu.SMEM)
    dma = pltpu.SemaphoreType.DMA
    scratch = (
        [pltpu.VMEM((ext_blocks, BLK, width), bf16) for _ in range(2 * chunks)]
        + [
            pltpu.VMEM((rows, columns), bf16),
            pltpu.VMEM((mem, columns), bf16),
            pltpu.VMEM((own, columns), bf16),
            pltpu.VMEM((mem // BLK, BLK, columns), bf16),
            pltpu.VMEM((mem // BLK, BLK, columns), bf16),
            pltpu.VMEM((rows, columns), bf16),
            pltpu.VMEM((own, columns), bf16),
            pltpu.VMEM((own, columns), f32),
            pltpu.VMEM((own, HD), f32),
            pltpu.VMEM((n, own, columns), bf16),
            pltpu.VMEM((n, 2 * heads, own), f32),
            pltpu.VMEM((n, own, columns), bf16),
            pltpu.VMEM((n, 2 * heads, own), f32),
        ]
        + [
            dma((5,)),
            dma((chunks, 2)),
            dma((chunks, 2, 2)),
            dma((chunks, 2, 2)),
            dma((n,)),
            dma((n,)),
            dma((n,)),
            dma((n,)),
            dma((chunks + 1,)),
        ]
    )

    def in_blocks(array):
        return array.reshape(-1, BLK, columns)

    return pl.pallas_call(
        functools.partial(kernel, n, heads, rows, mem, chunks),
        out_shape=(
            jax.ShapeDtypeStruct((rows, columns), bf16),
            jax.ShapeDtypeStruct((own, columns), bf16),
        ),
        in_specs=[smem_spec] * 2 + [any_spec] * 6,
        out_specs=(any_spec, any_spec),
        scratch_shapes=scratch,
        compiler_params=pltpu.CompilerParams(
            collective_id=0, has_side_effects=True, vmem_limit_bytes=60 << 20
        ),
        name="split_context_attention",
    )(
        window_blocks,
        memory_blocks,
        queries,
        in_blocks(keys),
        in_blocks(values),
        mem_queries,
        in_blocks(mem_keys),
        in_blocks(mem_values),
    )


def solution(mesh):
    in_specs = (
        P(("groups", "ctx"), ("head", "sub")),
        P(("groups", "ctx"), ("head", "sub")),
        P(("groups", "ctx"), ("head", "sub")),
        P("groups", ("head", "sub")),
        P("groups", ("head", "sub")),
        P("groups", ("head", "sub")),
        P(("groups", "ctx"), None),
        P(("groups", "ctx"), None),
    )
    out_specs = (P(("groups", "ctx"), ("head", "sub")), P(("groups", "ctx"), ("head", "sub")))
    return jax.shard_map(
        functools.partial(on_device, mesh.shape["ctx"]),
        mesh=mesh,
        in_specs=in_specs,
        out_specs=out_specs,
        check_vma=False,
    )
```

time: 173 us -> 44 us (0.25)
  blocking collectives: 87.8 us -> 0 us
  Pallas kernels: 0 us -> 40.6 us
  local copies, waits for them, and re-layouts: 32.2 us -> 2.56 us
  other arithmetic: 20.8 us -> 0 us
  between operations: 14.3 us -> 0.65 us
  matrix products: 8.99 us -> 0 us
  starting transfers between devices: 7.85 us -> 0 us
    all_gather x2 -> x0, blocking collectives: 87.8 us -> none  [joined_2(): pieces = jax.tree.map(lambda part: lax.all_gather(part, axis), value)]
    pallas_call x0 -> x1, Pallas kernels: none -> 40.6 us  [on_device(): pl.pallas_call(functools.partial(kernel, n, heads, rows, mem, chunks), ou...]
    dot_general x6 -> x0, matrix products: 8.99 us -> none  [the longest x1 2.63 us: on_device(): jnp.einsum('vfi,ifr->vfr', memory_exponents.astype(jnp.bfloat16), value_h...]
    ppermute x2 -> x0, starting transfers between devices: 7.81 us -> none  [the longest x1 6.53 us: with_halo(): lax.ppermute(lax.slice_in_dim(block, block.shape[dim] - width, None, axis...]
    select_n x3 -> x0, other arithmetic: 7.1 us -> none  [the longest x2 3.9 us: on_device(): memory_tiles = jnp.take(memory_pair, memory_blocks, axis=1)]
    gather x2 -> x0, local copies, waits for them, and re-layouts: 6.76 us -> none  [the longest x1 4.08 us: on_device(): near_tiles = jnp.take(extended, local_index, axis=1)]
    add x7 -> x0, other arithmetic: 6.61 us -> none  [the longest x3 6.47 us: combine_partials(): spread_factor_scale(first_sum, first_factor)]
    unnamed x32 -> x4, local copies, waits for them, and re-layouts: 9.08 us -> 2.56 us
  transfers between devices with their start and end apart: 3 -> 0, of which waited for: 0 -> 0; matrix products, arithmetic and copies ran while one was open for 21% -> 0% of each run, Pallas kernels for 0% -> 0%
where the time goes in v1:
time: 44 us; the launch traced here: 43.8 us
  Pallas kernels  40.6 us (92%)
  local copies, waits for them, and re-layouts  2.56 us (6%)
  between operations  0.65 us (1%)
    pallas_call x1, Pallas kernels, on_device(): pl.pallas_call(functools.partial(kernel, n, heads, rows, mem, chunks), ou...  40.6 us
    unnamed x4, local copies, waits for them, and re-layouts  2.56 us

profile of v1, /device:TPU:0, one launch (start us, length us, event | category | flops | bytes accessed | tf_op | source)
XLA Modules:
  0.0 43.8 jit_solution(12113287278576175270)
XLA Ops:
  0.6 40.6 %split_context_attention.1 = (bf16[256,1024]{1,0:T(8,128)(2,1)}, bf16[64,1024]{1,0:T(8,128)(2,1)}) custom-call(s32[4,5]{1,0:T(4,128)} %refs_0_.1, s32[4,3]{1,0:T(4,128)} %refs_1_.1, bf16[256,1024]{1,0:T(8,128)(2,1)} %refs_2_.1, bf16[4,64,1024]{2,1,0:T(8,128)(2,1)} %bitcast.4, bf16[4,64,1024]{2,1,0:T(8,128)(2,1)} %bitcast.5, bf16[256,1024]{1,0:T(8,128)(2,1)} %refs_5_.1, ...), custom_call_target="tpu_custom_call" | custom-call | tf_op jit(solution)/shard_map/split_context_attention/pallas_call | solution.py:358
  41.3 0.0 copy-start
  41.3 1.9 %copy.12 = bf16[256,1024]{1,0:T(8,128)(2,1)} copy(bf16[256,1024]{1,0:T(8,128)(2,1)} %get-tuple-element.4) | data formatting | bytes 1048576
  43.2 0.0 copy-done
  43.2 0.7 %copy.13 = bf16[64,1024]{1,0:T(8,128)(2,1)} copy(bf16[64,1024]{1,0:T(8,128)(2,1)S(1)} %copy-done) | data formatting | bytes 262144
Async XLA Ops:
  41.3 1.9 %copy-start = (bf16[64,1024]{1,0:T(8,128)(2,1)S(1)}, bf16[64,1024]{1,0:T(8,128)(2,1)}, u32[]{:S(2)}) copy-start(bf16[64,1024]{1,0:T(8,128)(2,1)} %get-tuple-element.5) | copy-start | bytes 393220

commit v2 on v1

v2 whole, which is shorter than its diff:
```python
import functools
import math

import jax
import jax.numpy as jnp
from jax import lax
from jax.experimental import pallas as pl
from jax.experimental.pallas import tpu as pltpu
from jax.sharding import PartitionSpec as P

HD = 128
BLK = 64
RADIUS = 4
MESH = pl.DeviceIdType.MESH
EXPONENT_SCALE = math.log2(math.e) / math.sqrt(HD)
LOWEST = -1e30
AHEAD = 3
PIECES = 4


def dot_nt(a, b):
    return lax.dot_general(a, b, (((1,), (1,)), ((), ())), preferred_element_type=jnp.float32)


def dot_nn(a, b):
    return lax.dot_general(a, b, (((1,), (0,)), ((), ())), preferred_element_type=jnp.float32)


def softmax_parts(scores):
    peak = jnp.max(scores, axis=1, keepdims=True)
    exps = jnp.exp2((scores - peak) * EXPONENT_SCALE)
    total = jnp.sum(exps, axis=1, keepdims=True)
    return peak, total, exps.astype(jnp.bfloat16)


def kernel(n, heads, rows, mem, groups, *refs):
    chunks = len(groups)
    (wb, mb, q_h, k_h, v_h, mq_h, mk_h, mv_h, out_h, mout_h) = refs[:10]
    refs = refs[10:]
    ext_k, ext_v, refs = refs[:chunks], refs[chunks : 2 * chunks], refs[2 * chunks :]
    (q_s, mq_s, mk_s, mv_s, out_s, mout_s, own_sum, own_stat, msg, msg_stat, got, got_stat) = refs[:12]
    (local_sem, kv_local, kv_send, kv_recv, p_send, p_recv, ps_send, ps_recv, out_sem) = refs[12:]

    def chunk_cols(c):
        return pl.ds(groups[c][0] * HD, groups[c][1] * HD)

    own = mem // n
    blocks = rows // BLK
    halo = RADIUS * BLK
    me = lax.axis_index("ctx")
    others = range(n // 2 - 1)
    has_low, has_high = me > 0, me < n - 1

    locals_ = [
        pltpu.make_async_copy(mq_h, mq_s, local_sem.at[0]),
        pltpu.make_async_copy(q_h, q_s, local_sem.at[1]),
        pltpu.make_async_copy(mk_h, mk_s, local_sem.at[2]),
        pltpu.make_async_copy(mv_h, mv_s, local_sem.at[3]),
    ]
    kv_locals = []
    for c in range(chunks):
        cols = chunk_cols(c)
        for t, (src, ext) in enumerate(((k_h, ext_k), (v_h, ext_v))):
            kv_locals.append(
                pltpu.make_async_copy(
                    src.at[:, :, cols], ext[c].at[pl.ds(RADIUS, blocks)], kv_local.at[c, t]
                )
            )
    locals_[0].start()
    for copy in kv_locals:
        copy.start()
    for copy in locals_[1:]:
        copy.start()

    barrier = pltpu.get_barrier_semaphore()
    for j in range(n):

        @pl.when(j != me)
        def _(j=j):
            pl.semaphore_signal(barrier, inc=1, device_id={"ctx": j}, device_id_type=MESH)

    pl.semaphore_wait(barrier, n - 1)

    high, low = jnp.minimum(me + 1, n - 1), jnp.maximum(me - 1, 0)

    def halo_copy(c, t, upward):
        src, ext = ((k_h, ext_k), (v_h, ext_v))[t]
        cols = chunk_cols(c)
        d = 0 if upward else 1
        if upward:
            part, start, target = pl.ds(blocks - RADIUS, RADIUS), 0, high
        else:
            part, start, target = pl.ds(0, RADIUS), RADIUS + blocks, low
        return pltpu.make_async_remote_copy(
            src_ref=src.at[part, :, cols],
            dst_ref=ext[c].at[pl.ds(start, RADIUS)],
            send_sem=kv_send.at[c, t, d],
            recv_sem=kv_recv.at[c, t, d],
            device_id={"ctx": target},
            device_id_type=MESH,
        )

    def send_halo(c):
        @pl.when(has_high)
        def _():
            for t in range(2):
                halo_copy(c, t, True).start()

        @pl.when(has_low)
        def _():
            for t in range(2):
                halo_copy(c, t, False).start()

    for c in range(min(AHEAD, chunks)):
        send_halo(c)

    @pl.when(jnp.logical_not(has_low))
    def _():
        for c in range(chunks):
            ext_k[c][0:RADIUS] = jnp.zeros((RADIUS,) + ext_k[c].shape[1:], jnp.bfloat16)
            ext_v[c][0:RADIUS] = jnp.zeros((RADIUS,) + ext_k[c].shape[1:], jnp.bfloat16)

    @pl.when(jnp.logical_not(has_high))
    def _():
        for c in range(chunks):
            ext_k[c][RADIUS + blocks :] = jnp.zeros((RADIUS,) + ext_k[c].shape[1:], jnp.bfloat16)
            ext_v[c][RADIUS + blocks :] = jnp.zeros((RADIUS,) + ext_k[c].shape[1:], jnp.bfloat16)

    def partial_copies(m, c):
        return (
            pltpu.make_async_remote_copy(
                src_ref=msg.at[m, :, chunk_cols(c)],
                dst_ref=got.at[m, :, chunk_cols(c)],
                send_sem=p_send.at[m, c],
                recv_sem=p_recv.at[m, c],
                device_id={"ctx": lax.rem(me + 2 * (m + 1), n)},
                device_id_type=MESH,
            ),
            pltpu.make_async_remote_copy(
                src_ref=msg_stat.at[m, c],
                dst_ref=got_stat.at[m, c],
                send_sem=ps_send.at[m, c],
                recv_sem=ps_recv.at[m, c],
                device_id={"ctx": lax.rem(me + 2 * (m + 1), n)},
                device_id_type=MESH,
            ),
        )

    for copy in kv_locals:
        copy.wait()
    for copy in locals_:
        copy.wait()

    half = lax.broadcasted_iota(jnp.int32, (1, halo + rows), 1)
    lane = lax.broadcasted_iota(jnp.int32, (own, HD), 1)

    def send_partials(c):
        first_head, count = groups[c]
        for m in range(len(others)):
            target = lax.rem(me + 2 * (m + 1), n)
            above = target > me
            start = jnp.where(above, 0, RADIUS)
            low_end = jnp.where(jnp.logical_and(above, jnp.logical_not(has_low)), halo, 0)
            high_end = jnp.where(
                jnp.logical_or(above, has_high), halo + rows, rows
            )
            valid = jnp.logical_and(half >= low_end, half < high_end)
            stats = jnp.zeros((own, HD), jnp.float32)
            for p in range(count):
                h, o = first_head + p, p * HD
                cols = slice(h * HD, (h + 1) * HD)
                span = pl.ds(start, RADIUS + blocks)
                key = ext_k[c][span, :, o : o + HD].reshape(halo + rows, HD)
                value = ext_v[c][span, :, o : o + HD].reshape(halo + rows, HD)
                scores = jnp.where(valid, dot_nt(mq_s[target, :, cols], key), LOWEST)
                peak, total, weights = softmax_parts(scores)
                msg[m, :, cols] = (dot_nn(weights, value) / total).astype(jnp.bfloat16)
                stats = jnp.where(lane == 2 * p, peak, stats)
                stats = jnp.where(lane == 2 * p + 1, total, stats)
            msg_stat[m, c] = stats.T[:8]
            for copy in partial_copies(m, c):
                copy.start()

    column = lax.broadcasted_iota(jnp.int32, (1, 2 * halo + rows + mem), 1)
    first = jnp.where(has_low, 0, halo)
    last = jnp.where(has_high, 2 * halo + rows, halo + rows)
    present = jnp.logical_or(
        jnp.logical_and(column >= first, column < last), column >= 2 * halo + rows
    )
    base = me * blocks - RADIUS

    def out_copy(c):
        cols = chunk_cols(c)
        return pltpu.make_async_copy(out_s.at[:, cols], out_h.at[:, cols], out_sem.at[c])

    def finish_memory(h):
        cols = slice(h * HD, (h + 1) * HD)
        mout_s[:, cols] = (own_sum[:, cols] / own_stat[:, heads + h : heads + h + 1]).astype(jnp.bfloat16)

    def fold_chunk(c):
        first_head, count = groups[c]
        for m in others:
            for copy in partial_copies(m, c):
                copy.wait_recv()
            columns = got_stat[m, c].T
            for p in range(count):
                h = first_head + p
                cols = slice(h * HD, (h + 1) * HD)
                peak, total = own_stat[:, h : h + 1], own_stat[:, heads + h : heads + h + 1]
                other_peak, other_total = columns[:, 2 * p : 2 * p + 1], columns[:, 2 * p + 1 : 2 * p + 2]
                joined = jnp.maximum(peak, other_peak)
                factor = jnp.exp2((peak - joined) * EXPONENT_SCALE)
                other = other_total * jnp.exp2((other_peak - joined) * EXPONENT_SCALE)
                own_sum[:, cols] = own_sum[:, cols] * factor + got[m, :, cols].astype(jnp.float32) * other
                own_stat[:, h : h + 1] = joined
                own_stat[:, heads + h : heads + h + 1] = total * factor + other
        for p in range(count):
            finish_memory(first_head + p)

    for c in range(chunks):
        @pl.when(has_low)
        def _(c=c):
            for t in range(2):
                halo_copy(c, t, True).wait_recv()

        @pl.when(has_high)
        def _(c=c):
            for t in range(2):
                halo_copy(c, t, False).wait_recv()

        send_partials(c)
        if c + AHEAD < chunks:
            send_halo(c + AHEAD)
        for p in range(groups[c][1]):
            h, o = groups[c][0] + p, p * HD
            cols = slice(h * HD, (h + 1) * HD)
            for b in range(blocks):
                near = [
                    jnp.clip(wb[b, s] - base, 0, blocks + 2 * RADIUS - 1) for s in range(wb.shape[1])
                ]
                distant = [jnp.clip(mb[b, s], 0, mem // BLK - 1) for s in range(mb.shape[1])]
                key = jnp.concatenate(
                    [ext_k[c][s, :, o : o + HD] for s in near]
                    + [mk_s[s, :, cols] for s in distant],
                    axis=0,
                )
                value = jnp.concatenate(
                    [ext_v[c][s, :, o : o + HD] for s in near]
                    + [mv_s[s, :, cols] for s in distant],
                    axis=0,
                )
                part = slice(b * BLK, (b + 1) * BLK)
                peak, total, weights = softmax_parts(dot_nt(q_s[part, cols], key))
                out_s[part, cols] = (dot_nn(weights, value) / total).astype(jnp.bfloat16)
            query = mq_s[me, :, cols]
            key = jnp.concatenate(
                [
                    ext_k[c][:, :, o : o + HD].reshape(rows + 2 * halo, HD),
                    mk_s[:, :, cols].reshape(mem, HD),
                ],
                axis=0,
            )
            value = jnp.concatenate(
                [
                    ext_v[c][:, :, o : o + HD].reshape(rows + 2 * halo, HD),
                    mv_s[:, :, cols].reshape(mem, HD),
                ],
                axis=0,
            )
            scores = jnp.where(present, dot_nt(query, key), LOWEST)
            peak, total, weights = softmax_parts(scores)
            own_sum[:, cols] = dot_nn(weights, value)
            own_stat[:, h : h + 1] = peak
            own_stat[:, heads + h : heads + h + 1] = total
        out_copy(c).start()
        if c == chunks - 1:
            for earlier in range(c):
                fold_chunk(earlier)

    fold_chunk(chunks - 1)
    mem_out = pltpu.make_async_copy(mout_s, mout_h, out_sem.at[chunks])
    mem_out.start()

    for c in range(chunks):

        @pl.when(has_high)
        def _(c=c):
            for t in range(2):
                halo_copy(c, t, True).wait_send()

        @pl.when(has_low)
        def _(c=c):
            for t in range(2):
                halo_copy(c, t, False).wait_send()

        for m in others:
            for copy in partial_copies(m, c):
                copy.wait_send()
        out_copy(c).wait()
    mem_out.wait()


def place(a_ref, m_ref, a_out, m_out, sems):
    part = a_ref.shape[0] // PIECES
    copies = [
        pltpu.make_async_copy(
            a_ref.at[pl.ds(i * part, part)], a_out.at[pl.ds(i * part, part)], sems.at[i]
        )
        for i in range(PIECES)
    ] + [pltpu.make_async_copy(m_ref, m_out, sems.at[PIECES])]
    for copy in copies:
        copy.start()
    for copy in copies:
        copy.wait()


def on_device(
    n, queries, keys, values, mem_queries, mem_keys, mem_values, window_blocks, memory_blocks
):
    rows, columns = queries.shape
    mem = mem_queries.shape[0]
    heads = columns // HD
    sizes = [2] * ((heads - 2) // 2) + [1, 1]
    groups = [(sum(sizes[:c]), size) for c, size in enumerate(sizes)]
    chunks, far = len(groups), n // 2 - 1
    own = mem // n
    ext_blocks = rows // BLK + 2 * RADIUS
    bf16, f32 = jnp.bfloat16, jnp.float32
    any_spec = pl.BlockSpec(memory_space=pl.ANY)
    smem_spec = pl.BlockSpec(memory_space=pltpu.SMEM)
    dma = pltpu.SemaphoreType.DMA
    scratch = (
        [pltpu.VMEM((ext_blocks, BLK, size * HD), bf16) for _ in range(2) for size in sizes]
        + [
            pltpu.VMEM((rows, columns), bf16),
            pltpu.VMEM((n, own, columns), bf16),
            pltpu.VMEM((mem // BLK, BLK, columns), bf16),
            pltpu.VMEM((mem // BLK, BLK, columns), bf16),
            pltpu.VMEM((rows, columns), bf16),
            pltpu.VMEM((own, columns), bf16),
            pltpu.VMEM((own, columns), f32),
            pltpu.VMEM((own, HD), f32),
            pltpu.VMEM((far, own, columns), bf16),
            pltpu.VMEM((far, chunks, 8, own), f32),
            pltpu.VMEM((far, own, columns), bf16),
            pltpu.VMEM((far, chunks, 8, own), f32),
        ]
        + [
            dma((4,)),
            dma((chunks, 2)),
            dma((chunks, 2, 2)),
            dma((chunks, 2, 2)),
            dma((far, chunks)),
            dma((far, chunks)),
            dma((far, chunks)),
            dma((far, chunks)),
            dma((chunks + 1,)),
        ]
    )

    def in_blocks(array):
        return array.reshape(-1, BLK, columns)

    attended, memory_out = pl.pallas_call(
        functools.partial(kernel, n, heads, rows, mem, groups),
        out_shape=(
            jax.ShapeDtypeStruct((rows, columns), bf16),
            jax.ShapeDtypeStruct((own, columns), bf16),
        ),
        in_specs=[smem_spec] * 2 + [any_spec] * 6,
        out_specs=(any_spec, any_spec),
        scratch_shapes=scratch,
        compiler_params=pltpu.CompilerParams(
            collective_id=0, has_side_effects=True, vmem_limit_bytes=60 << 20
        ),
        name="split_context_attention",
    )(
        window_blocks,
        memory_blocks,
        queries,
        in_blocks(keys),
        in_blocks(values),
        mem_queries.reshape(n, own, columns),
        in_blocks(mem_keys),
        in_blocks(mem_values),
    )
    return pl.pallas_call(
        place,
        out_shape=(
            jax.ShapeDtypeStruct((rows, columns), bf16),
            jax.ShapeDtypeStruct((own, columns), bf16),
        ),
        in_specs=[any_spec] * 2,
        out_specs=(any_spec, any_spec),
        scratch_shapes=[dma((PIECES + 1,))],
        compiler_params=pltpu.CompilerParams(vmem_limit_bytes=60 << 20),
        name="place",
    )(attended, memory_out)


def solution(mesh):
    in_specs = (
        P(("groups", "ctx"), ("head", "sub")),
        P(("groups", "ctx"), ("head", "sub")),
        P(("groups", "ctx"), ("head", "sub")),
        P("groups", ("head", "sub")),
        P("groups", ("head", "sub")),
        P("groups", ("head", "sub")),
        P(("groups", "ctx"), None),
        P(("groups", "ctx"), None),
    )
    out_specs = (P(("groups", "ctx"), ("head", "sub")), P(("groups", "ctx"), ("head", "sub")))
    return jax.shard_map(
        functools.partial(on_device, mesh.shape["ctx"]),
        mesh=mesh,
        in_specs=in_specs,
        out_specs=out_specs,
        check_vma=False,
    )
```

time: 44 us -> 62.2 us (1.41)
  Pallas kernels: 40.6 us -> 61.4 us
  local copies, waits for them, and re-layouts: 2.56 us -> 0 us
    pallas_call x1 -> x2, Pallas kernels: 40.6 us -> 61.4 us  [the longest x1 40.4 us: on_device(): pl.pallas_call(functools.partial(kernel, n, heads, rows, mem, groups), ou...]
    unnamed x4 -> x0, local copies, waits for them, and re-layouts: 2.56 us -> none
where the time goes in v2:
time: 62.2 us; the launch traced here: 62 us
  Pallas kernels  61.4 us (99%)
  between operations  0.64 us (1%)
    pallas_call x1, Pallas kernels, on_device(): pl.pallas_call(functools.partial(kernel, n, heads, rows, mem, groups), ou...  40.4 us
    pallas_call x1, Pallas kernels, on_device(): pl.pallas_call(place, out_shape=(jax.ShapeDtypeStruct((rows, columns), bf...  21 us

profile of v2, /device:TPU:0, one launch (start us, length us, event | category | flops | bytes accessed | tf_op | source)
XLA Modules:
  0.0 62.0 jit_solution(7042736532970562894)
XLA Ops:
  0.6 40.4 %split_context_attention.1 = (bf16[256,1024]{1,0:T(8,128)(2,1)}, bf16[64,1024]{1,0:T(8,128)(2,1)}) custom-call(s32[4,5]{1,0:T(4,128)} %refs_0_.1, s32[4,3]{1,0:T(4,128)} %refs_1_.1, bf16[256,1024]{1,0:T(8,128)(2,1)} %refs_2_.1, bf16[4,64,1024]{2,1,0:T(8,128)(2,1)} %bitcast.5, bf16[4,64,1024]{2,1,0:T(8,128)(2,1)} %bitcast.6, bf16[4,64,1024]{2,1,0:T(8,128)(2,1)} %bitcast.7, ...), custom_call_target="tpu_custom_call" | custom-call | tf_op jit(solution)/shard_map/split_context_attention/pallas_call | solution.py:364
  41.0 21.0 %place.1 = (bf16[256,1024]{1,0:T(8,128)(2,1)}, bf16[64,1024]{1,0:T(8,128)(2,1)}) custom-call(bf16[256,1024]{1,0:T(8,128)(2,1)} %get-tuple-element.4.a_ref, bf16[64,1024]{1,0:T(8,128)(2,1)} %get-tuple-element.5.m_ref), custom_call_target="tpu_custom_call" | custom-call | tf_op jit(solution)/shard_map/place/pallas_call | solution.py:387

commit v3 on v2

--- a/solution.py
+++ b/solution.py
@@ -14,7 +14,7 @@
 MESH = pl.DeviceIdType.MESH
 EXPONENT_SCALE = math.log2(math.e) / math.sqrt(HD)
 LOWEST = -1e30
-AHEAD = 3
+AHEAD = 8
 PIECES = 4
 
 
@@ -300,17 +300,21 @@
     mem_out.wait()
 
 
-def place(a_ref, m_ref, a_out, m_out, sems):
+def place(a_ref, m_ref, a_out, m_out, a_s, m_s, sems):
     part = a_ref.shape[0] // PIECES
-    copies = [
-        pltpu.make_async_copy(
-            a_ref.at[pl.ds(i * part, part)], a_out.at[pl.ds(i * part, part)], sems.at[i]
-        )
+    spans = [
+        (ref.at[pl.ds(i * part, part)], held.at[pl.ds(i * part, part)], out.at[pl.ds(i * part, part)])
+        for ref, held, out in ((a_ref, a_s, a_out),)
         for i in range(PIECES)
-    ] + [pltpu.make_async_copy(m_ref, m_out, sems.at[PIECES])]
-    for copy in copies:
+    ] + [(m_ref, m_s, m_out)]
+    loads = [pltpu.make_async_copy(x, y, sems.at[0, i]) for i, (x, y, _) in enumerate(spans)]
+    stores = [pltpu.make_async_copy(y, z, sems.at[1, i]) for i, (_, y, z) in enumerate(spans)]
+    for copy in loads:
         copy.start()
-    for copy in copies:
+    for load, store in zip(loads, stores):
+        load.wait()
+        store.start()
+    for copy in stores:
         copy.wait()
 
 
@@ -392,7 +396,11 @@
         ),
         in_specs=[any_spec] * 2,
         out_specs=(any_spec, any_spec),
-        scratch_shapes=[dma((PIECES + 1,))],
+        scratch_shapes=[
+            pltpu.VMEM((rows, columns), bf16),
+            pltpu.VMEM((own, columns), bf16),
+            dma((2, PIECES + 1)),
+        ],
         compiler_params=pltpu.CompilerParams(vmem_limit_bytes=60 << 20),
         name="place",
     )(attended, memory_out)

time: 62.2 us -> 41.8 us (0.67)
  Pallas kernels: 61.4 us -> 41 us
    pallas_call x1, Pallas kernels: 21 us -> 1.91 us  [on_device(): pl.pallas_call(place, out_shape=(jax.ShapeDtypeStruct((rows, columns), bf...]
    pallas_call x1, Pallas kernels: 40.4 us -> 39.1 us  [on_device(): pl.pallas_call(functools.partial(kernel, n, heads, rows, mem, groups), ou...]
where the time goes in v3:
time: 41.8 us; the launch traced here: 41.7 us
  Pallas kernels  41 us (98%)
  between operations  0.64 us (2%)
    pallas_call x1, Pallas kernels, on_device(): pl.pallas_call(functools.partial(kernel, n, heads, rows, mem, groups), ou...  39.1 us
    pallas_call x1, Pallas kernels, on_device(): pl.pallas_call(place, out_shape=(jax.ShapeDtypeStruct((rows, columns), bf...  1.91 us

profile of v3, /device:TPU:0, one launch (start us, length us, event | category | flops | bytes accessed | tf_op | source)
XLA Modules:
  0.0 41.7 jit_solution(3247737914348003258)
XLA Ops:
  0.6 39.1 %split_context_attention.1 = (bf16[256,1024]{1,0:T(8,128)(2,1)}, bf16[64,1024]{1,0:T(8,128)(2,1)}) custom-call(s32[4,5]{1,0:T(4,128)} %refs_0_.1, s32[4,3]{1,0:T(4,128)} %refs_1_.1, bf16[256,1024]{1,0:T(8,128)(2,1)} %refs_2_.1, bf16[4,64,1024]{2,1,0:T(8,128)(2,1)} %bitcast.5, bf16[4,64,1024]{2,1,0:T(8,128)(2,1)} %bitcast.6, bf16[4,64,1024]{2,1,0:T(8,128)(2,1)} %bitcast.7, ...), custom_call_target="tpu_custom_call" | custom-call | tf_op jit(solution)/shard_map/split_context_attention/pallas_call | solution.py:368
  39.8 1.9 %place.1 = (bf16[256,1024]{1,0:T(8,128)(2,1)}, bf16[64,1024]{1,0:T(8,128)(2,1)}) custom-call(bf16[256,1024]{1,0:T(8,128)(2,1)} %get-tuple-element.4.a_ref, bf16[64,1024]{1,0:T(8,128)(2,1)} %get-tuple-element.5.m_ref), custom_call_target="tpu_custom_call" | custom-call | tf_op jit(solution)/shard_map/place/pallas_call | solution.py:391

commit v4 on v3

--- a/solution.py
+++ b/solution.py
@@ -14,7 +14,7 @@
 MESH = pl.DeviceIdType.MESH
 EXPONENT_SCALE = math.log2(math.e) / math.sqrt(HD)
 LOWEST = -1e30
-AHEAD = 8
+AHEAD = 3
 PIECES = 4
 
 
@@ -111,8 +111,14 @@
             for t in range(2):
                 halo_copy(c, t, False).start()
 
+    paced = lax.axis_index("sub") > 0
     for c in range(min(AHEAD, chunks)):
         send_halo(c)
+
+    @pl.when(jnp.logical_not(paced))
+    def _():
+        for c in range(AHEAD, chunks):
+            send_halo(c)
 
     @pl.when(jnp.logical_not(has_low))
     def _():
@@ -230,7 +236,11 @@
 
         send_partials(c)
         if c + AHEAD < chunks:
-            send_halo(c + AHEAD)
+
+            @pl.when(paced)
+            def _(c=c):
+                send_halo(c + AHEAD)
+
         for p in range(groups[c][1]):
             h, o = groups[c][0] + p, p * HD
             cols = slice(h * HD, (h + 1) * HD)

time: 41.8 us -> 41.8 us (level)
  no operation moved by 1% of the time
where the time goes in v4:
time: 41.8 us; the launch traced here: 41.7 us
  Pallas kernels  41 us (98%)
  between operations  0.64 us (2%)
    pallas_call x1, Pallas kernels, on_device(): pl.pallas_call(functools.partial(kernel, n, heads, rows, mem, groups), ou...  39.1 us
    pallas_call x1, Pallas kernels, on_device(): pl.pallas_call(place, out_shape=(jax.ShapeDtypeStruct((rows, columns), bf...  1.91 us

profile of v4, /device:TPU:0, one launch (start us, length us, event | category | flops | bytes accessed | tf_op | source)
XLA Modules:
  0.0 41.7 jit_solution(4155324515703818693)
XLA Ops:
  0.6 39.1 %split_context_attention.1 = (bf16[256,1024]{1,0:T(8,128)(2,1)}, bf16[64,1024]{1,0:T(8,128)(2,1)}) custom-call(s32[4,5]{1,0:T(4,128)} %refs_0_.1, s32[4,3]{1,0:T(4,128)} %refs_1_.1, bf16[256,1024]{1,0:T(8,128)(2,1)} %refs_2_.1, bf16[4,64,1024]{2,1,0:T(8,128)(2,1)} %bitcast.5, bf16[4,64,1024]{2,1,0:T(8,128)(2,1)} %bitcast.6, bf16[4,64,1024]{2,1,0:T(8,128)(2,1)} %bitcast.7, ...), custom_call_target="tpu_custom_call" | custom-call | tf_op jit(solution)/shard_map/split_context_attention/pallas_call | solution.py:378
  39.8 1.9 %place.1 = (bf16[256,1024]{1,0:T(8,128)(2,1)}, bf16[64,1024]{1,0:T(8,128)(2,1)}) custom-call(bf16[256,1024]{1,0:T(8,128)(2,1)} %get-tuple-element.4.a_ref, bf16[64,1024]{1,0:T(8,128)(2,1)} %get-tuple-element.5.m_ref), custom_call_target="tpu_custom_call" | custom-call | tf_op jit(solution)/shard_map/place/pallas_call | solution.py:401
